TPU v7x, 32 devices: a whole 2x2x4 slice. The times are simulated.
32 devices in a mesh: seq: 4 (over y, x), tp: 8 (over z, core).
Axes of the slice: x: 2, y: 2, z: 4, core: 2. Of those that a mesh axis runs over, the one named last changes fastest.
Arguments:
- tokens: bfloat16 [1, 512, 4096], P(None, 'seq', 'tp'), may hold values from -6 to 6
- projections: bfloat16 [4096, 3, 4096], P(None, None, 'tp'), may hold values from -1.5 to 1.5
- out_weight: bfloat16 [4096, 4096], P('tp'), may hold values from -0.09375 to 0.09375
- gain_in: float32 [4096], P('tp'), may hold values from 0.5 to 1.5
- gain_out: float32 [4096], P('tp'), may hold values from 0.5 to 1.5
- iterates: float32 [5, 1, 512, 4096], P(None, None, 'seq', 'tp'), may hold values from -5 to 5
- images: float32 [5, 1, 512, 4096], P(None, None, 'seq', 'tp'), may hold values from -330 to 330
Outputs:
- mixed: float32 [1, 512, 4096], P(None, 'seq', 'tp')
- image: float32 [1, 512, 4096], P(None, 'seq', 'tp')
All inputs are finite; a program needn't handle non-finite values.
Results may differ from a plain program's by a relative error of at most 0.013.
Values may be sent and summed in bfloat16 or wider, within the bound.
No kernel may reach another device: no remote copies, remote signals or barrier semaphores. Data moves between devices by JAX's collectives and lax.ppermute only.
A program may use at most 64 MiB of HBM per device.

v0:
```python
import jax
import jax.numpy as jnp
from jax import lax
from jax.sharding import PartitionSpec as P

HEAD_SIZE = 128
ITERS = 2
epsilon = 1e-05
rope_base = 10000.0
ridge_factor = 0.01


def rotate(vectors, positions):
    half_dim = vectors.shape[-1] // 2
    frequency = rope_base ** (-2.0 * jnp.arange(half_dim).astype(jnp.float32) / vectors.shape[-1])
    angles = positions[:, None] * frequency[None, :]
    cosine = jnp.cos(angles)
    sine_part = jnp.sin(angles)
    first_half = vectors[..., :half_dim]
    second_half = vectors[..., half_dim:]
    return jnp.concatenate(
        [
            first_half * cosine - second_half * sine_part,
            second_half * cosine + first_half * sine_part,
        ],
        axis=-1,
    )


def solve_small(matrix, target):
    extent = matrix.shape[0]
    indices = jnp.arange(extent)
    for column in range(extent):
        factor = jnp.where(indices > column, matrix[:, column] / matrix[column, column], 0.0)
        matrix = matrix - factor[:, None] * matrix[column][None, :]
        target = target - factor * target[column]
    answer = jnp.zeros_like(target)
    for column in reversed(range(extent)):
        entry_value = (target[column] - jnp.sum(matrix[column] * answer)) / matrix[column, column]
        answer = answer.at[column].set(entry_value)
    return answer


def anderson_weights(gram):
    extent = gram.shape[0]
    ridge = ridge_factor * jnp.trace(gram) / extent
    regular = gram + ridge * jnp.eye(extent, dtype=gram.dtype)
    solved = solve_small(regular, jnp.ones((extent,), gram.dtype))
    return solved / jnp.sum(solved)


def pair_products(left, right):
    return jnp.einsum("mbsd,nbsd->mn", left, right, precision=lax.Precision.HIGHEST)


def grow_gram(gram, new_row, own_value):
    upper = jnp.concatenate([gram[1:, 1:], new_row[:, None]], axis=1)
    lower = jnp.concatenate([new_row, own_value[None]])[None, :]
    return jnp.concatenate([upper, lower], axis=0)


def shards(tokens, projections, out_weight, gain_in, gain_out, iterates, images):
    batch_count, local_length, local_width = tokens.shape
    full_width = local_width * lax.axis_size("tp")
    heads = projections.shape[2] // HEAD_SIZE
    seq_start = lax.axis_index("seq") * local_length
    query_index = seq_start + jnp.arange(local_length, dtype=jnp.int32)
    positions = query_index.astype(jnp.float32)
    score_scale = HEAD_SIZE ** (-0.5)
    residuals = images - iterates
    gram = lax.psum(pair_products(residuals, residuals), ("seq", "tp"))
    mixed = iterates[0]
    image = images[0]
    for step_index in range(ITERS):
        alpha = anderson_weights(gram)
        mixed = jnp.einsum("m,mbsd->bsd", alpha, images, precision=lax.Precision.HIGHEST)
        layer_squares = lax.psum(jnp.sum(mixed * mixed, axis=-1), "tp")
        layer_row_scale = lax.rsqrt(layer_squares / full_width + epsilon)
        normed = (mixed * layer_row_scale[..., None] * gain_in).astype(jnp.bfloat16)
        empty = jnp.zeros((batch_count, local_length, 3, projections.shape[2]), jnp.float32)
        piece = lax.all_gather(normed, "tp", axis=2, tiled=True)
        rows = lax.slice_in_dim(projections, 0, piece.shape[2], axis=0)
        mapped = empty + jnp.einsum(
            "bsd,dce->bsce", piece, rows, preferred_element_type=jnp.float32
        )
        pieces = mapped.reshape(batch_count, local_length, 3, heads, HEAD_SIZE).transpose(
            2, 0, 3, 1, 4
        )
        query_rows = rotate(pieces[0], positions).astype(jnp.bfloat16)
        key_rows = rotate(pieces[1], positions).astype(jnp.bfloat16)
        value_rows = pieces[2].astype(jnp.bfloat16)
        row_shape = (batch_count, heads, local_length)
        best = jnp.full(row_shape, -1e30, jnp.float32)
        key_piece = lax.all_gather(key_rows, "seq", axis=2, tiled=True)
        value_piece = lax.all_gather(value_rows, "seq", axis=2, tiled=True)
        logit_scores = (
            jnp.einsum("bhqd,bhkd->bhqk", query_rows, key_piece, preferred_element_type=jnp.float32)
            * score_scale
        )
        key_index = jnp.arange(key_piece.shape[2], dtype=jnp.int32)
        allowed = key_index[None, :] <= query_index[:, None]
        logit_scores = jnp.where(allowed, logit_scores, -1e30)
        newest = jnp.maximum(best, jnp.max(logit_scores, axis=-1))
        softmax_weights = jnp.where(allowed, jnp.exp(logit_scores - newest[..., None]), 0.0)
        total = jnp.sum(softmax_weights, axis=-1)
        accum = jnp.einsum(
            "bhqk,bhkd->bhqd",
            softmax_weights.astype(jnp.bfloat16),
            value_piece,
            preferred_element_type=jnp.float32,
        )
        best, total, accum = (newest, total, accum)
        attended = (
            (accum / total[..., None])
            .astype(jnp.bfloat16)
            .transpose(0, 2, 1, 3)
            .reshape(batch_count, local_length, heads * HEAD_SIZE)
        )
        partial_value = jnp.einsum(
            "bse,ed->bsd", attended, out_weight, preferred_element_type=jnp.float32
        )
        attention = lax.psum_scatter(
            partial_value.astype(jnp.bfloat16), "tp", scatter_dimension=2, tiled=True
        ).astype(jnp.float32)
        layer_summed = tokens.astype(jnp.float32) + attention
        scaled = layer_summed * gain_out
        if step_index + 1 == ITERS:
            finish_squares = lax.psum(jnp.sum(layer_summed * layer_summed, axis=-1), "tp")
            image = scaled * lax.rsqrt(finish_squares / full_width + epsilon)[..., None]
        else:
            advance_gram = gram
            advance_residuals = residuals
            kept = advance_residuals[1:]
            cross_scaled = jnp.einsum(
                "bsd,mbsd->mbs", scaled, kept, precision=lax.Precision.HIGHEST
            )
            cross_mixed = jnp.einsum("bsd,mbsd->mbs", mixed, kept, precision=lax.Precision.HIGHEST)
            totals = lax.psum(
                (
                    jnp.sum(layer_summed * layer_summed, axis=-1),
                    cross_scaled,
                    cross_mixed,
                    jnp.sum(scaled * scaled, axis=-1),
                    jnp.sum(scaled * mixed, axis=-1),
                    jnp.sum(mixed * mixed, axis=-1),
                ),
                "tp",
            )
            squares, scaled_cross, mixed_cross, scaled_own, joint_own, mixed_own = totals
            row_scale = lax.rsqrt(squares / full_width + epsilon)
            advance_image = scaled * row_scale[..., None]
            row_terms = jnp.sum(row_scale[None] * scaled_cross - mixed_cross, axis=(1, 2))
            own_terms = jnp.sum(
                row_scale * row_scale * scaled_own - 2.0 * row_scale * joint_own + mixed_own
            )
            new_row, own_value = lax.psum((row_terms, own_terms), "seq")
            advance_residuals = jnp.concatenate([kept, (advance_image - mixed)[None]], axis=0)
            advance_gram = grow_gram(advance_gram, new_row, own_value)
            image = advance_image
            residuals = advance_residuals
            gram = advance_gram
            images = jnp.concatenate([images[1:], image[None]], axis=0)
    return (mixed, image)


def solution(mesh):
    in_specs = (
        P(None, "seq", "tp"),
        P(None, None, "tp"),
        P("tp", None),
        P("tp"),
        P("tp"),
        P(None, None, "seq", "tp"),
        P(None, None, "seq", "tp"),
    )
    out_specs = (P(None, "seq", "tp"), P(None, "seq", "tp"))
    return jax.shard_map(shards, mesh=mesh, in_specs=in_specs, out_specs=out_specs, check_vma=False)
```

profile of v0, /device:TPU:0, one launch (start us, length us, event | category | flops | bytes accessed | tf_op | source)
XLA Modules:
  0.0 377.3 jit_solution(1337387105630204352)
XLA Ops:
  7.2 2.0 sub.129
  9.2 1.1 copy-done.3
  10.3 1.0 copy.29
  11.3 5.0 %convolution_bitcast_fusion.1 = f32[5,5]{1,0:T(8,128)S(1)} fusion(f32[5,128,512]{1,0,2:T(8,128)S(1)} %copy.29), kind=kOutput, calls=%fused_computation.18 | convolution fusion | flops 19660800 | bytes 1310820 | tf_op jit(solution)/shard_map/mbsd,nbsd->mn/dot_general | solution.py:53
  16.3 42.0 %psum.80 = f32[5,5]{1,0:T(8,128)S(1)} all-reduce(f32[5,5]{1,0:T(8,128)S(1)} %convolution_bitcast_fusion.1), channel_id=1, replica_groups=mesh['seq'=4,'tp'=8] {'seq','tp'}, use_global_device_ids=true, to_apply=%region_0.0 | all-reduce | flops 25 | bytes 200 | tf_op jit(solution)/shard_map/psum | solution.py:71
  60.0 0.8 fusion.53
  61.5 0.8 select_reduce_fusion.9
  63.0 0.8 select_reduce_fusion.8
  64.5 0.8 select_reduce_fusion.7
  66.0 0.8 select_reduce_fusion.6
  66.9 0.7 fusion.102
  68.7 0.6 fusion.66
  70.0 0.6 fusion.70
  71.2 0.6 fusion.74
  72.5 0.6 fusion.78
  73.1 0.7 fusion.104
  75.7 0.7 fusion.90
  78.3 0.7 fusion.89
  80.9 0.6 fusion.88
  86.7 3.2 fusion.4
  90.0 14.4 %psum.81 = f32[1,128]{1,0:T(1,128)S(1)} all-reduce(f32[1,128]{1,0:T(1,128)S(1)} %bitcast.256), channel_id=1, replica_groups=mesh['seq'=4,'tp'=8] {'tp'}, use_global_device_ids=true, to_apply=%region_9.10 | all-reduce | flops 128 | bytes 1024 | tf_op jit(solution)/shard_map/psum | solution.py:77
  104.5 0.8 fusion.38
  105.3 17.0 %copy.54 = bf16[3,512,4096]{2,1,0:T(8,128)(2,1)} copy(bf16[3,512,4096]{1,2,0:T(8,128)(2,1)} %bitcast.243) | data formatting | bytes 25165824 | tf_op jit(solution)/shard_map/bsd,dce->bsce/dot_general | solution.py:83
  122.6 3.1 all-gather.7.cloned.1.call-done
  125.7 6.7 %fusion.11 = f32[128,3,4,128]{0,3,2,1:T(8,128)S(1)} fusion(bf16[3,4,128,4096]{3,2,1,0:T(8,128)(2,1)} %bitcast.240, bf16[128,4096]{1,0:T(8,128)(2,1)} %all-gather.7.cloned.1.call-done), kind=kOutput, calls=%fused_computation.21 | convolution fusion | flops 1610612736 | bytes 14417920 | tf_op jit(solution)/shard_map/bsd,dce->bsce/dot_general | solution.py:83
  132.6 10.0 %all_gather.19 = bf16[1,4,512,128]{2,3,1,0:T(8,128)(2,1)S(1)} all-gather(bf16[1,4,128,128]{2,3,1,0:T(8,128)(2,1)S(1)} %pad_maximum_fusion), channel_id=1, replica_groups=mesh['seq'=4,'tp'=8] {'seq'}, dimensions={2}, use_global_device_ids=true | all-gather | bytes 655360 | tf_op jit(solution)/shard_map/all_gather | solution.py:94
  143.1 11.0 %all-gather.1 = bf16[1,1,4,512,128]{3,4,2,0,1:T(8,128)(2,1)S(1)} all-gather(bf16[1,1,4,128,128]{3,4,2,0,1:T(8,128)(2,1)S(1)} %slice.565), channel_id=3, replica_groups=mesh['seq'=4,'tp'=8] {'seq'}, dimensions={3}, use_global_device_ids=true | all-gather | bytes 655360 | tf_op jit(solution)/shard_map/all_gather | solution.py:95
  154.8 1.7 fusion
  156.7 1.0 slice.432
  158.3 1.1 slice_bitcast_fusion
  159.4 28.7 %reduce-scatter.3.cloned.1.call-done = bf16[1,128,512]{2,1,0:T(8,128)(2,1)} async-done(((bf16[1,128,4096]{2,1,0:T(8,128)(2,1)}), bf16[1,128,512]{2,1,0:T(8,128)(2,1)}) %reduce-scatter.3.cloned.1.call-update) | async-done | bytes 131088 | tf_op jit(solution)/shard_map/reduce_scatter | solution.py:122
  188.1 1.1 multiply_reduce_fusion.2
  189.2 5.9 %fusion.15 = f32[128,1,4]{2,1,0:T(1,128)S(1)} fusion(f32[4,128,512]{2,1,0:T(8,128)} %slice_bitcast_fusion, f32[128,512,1]{1,0,2:T(8,128)S(1)} %get-tuple-element.164), kind=kOutput, calls=%fused_computation.27 | convolution fusion | flops 3145728 | bytes 1312768 | tf_op jit(solution)/shard_map/bsd,mbsd->mbs/dot_general | solution.py:134
  195.2 4.6 %fusion.13 = f32[128,1,4]{2,1,0:T(1,128)S(1)} fusion(f32[4,128,512]{2,1,0:T(8,128)S(1)} %copy-done.8, f32[128,512,1]{1,0,2:T(8,128)S(1)} %get-tuple-element.165), kind=kOutput, calls=%fused_computation.25 | convolution fusion | flops 3145728 | bytes 1312768 | tf_op jit(solution)/shard_map/bsd,mbsd->mbs/dot_general | solution.py:137
  199.8 13.9 %all-reduce.2 = (f32[1,128]{1,0:T(1,128)S(1)}, f32[1,128]{1,0:T(1,128)S(1)}, f32[1,128]{1,0:T(1,128)S(1)}, f32[4,1,128]{2,0,1:T(4,128)S(1)}, f32[4,1,128]{2,0,1:T(4,128)S(1)}) all-reduce(f32[1,128]{1,0:T(1,128)S(1)} %bitcast.254, f32[1,128]{1,0:T(1,128)S(1)} %bitcast.253, ...), channel_id=1, replica_groups=mesh['seq'=4,'tp'=8] {'tp'}, use_global_device_ids=true, to_apply=%region_14.15 | all-reduce | flops 1408 | bytes 11264 | tf_op jit(solution)/shard_map/psum | solution.py:138
  214.5 11.1 %all-reduce.3 = (f32[1]{0:T(128)}, f32[4]{0:T(128)S(1)}) all-reduce(f32[1]{0:T(128)} %bitcast.72, f32[4]{0:T(128)S(1)} %subtract_reduce_fusion), channel_id=1, replica_groups=mesh['seq'=4,'tp'=8] {'seq'}, use_global_device_ids=true, to_apply=%region_24.25 | all-reduce | flops 5 | bytes 40 | tf_op jit(solution)/shard_map/psum | solution.py:156
  225.6 0.7 maximum_bitcast_fusion.1
  226.4 0.7 select_reduce_fusion.5
  228.3 0.8 fusion.58
  229.8 0.8 select_reduce_fusion.3
  231.3 0.8 select_reduce_fusion.2
  232.8 0.8 select_reduce_fusion.1
  234.3 0.8 select_reduce_fusion
  235.2 0.7 fusion.101
  237.1 0.6 fusion.68
  238.3 0.6 fusion.72
  239.5 0.6 fusion.76
  240.8 0.6 fusion.80
  241.4 0.6 fusion.103
  244.0 0.8 fusion.85
  246.9 0.7 fusion.84
  249.6 0.7 fusion.83
  255.6 3.2 fusion.2
  259.0 13.6 %psum.89 = f32[1,128]{1,0:T(1,128)S(1)} all-reduce(f32[1,128]{1,0:T(1,128)S(1)} %bitcast.255), channel_id=1, replica_groups=mesh['seq'=4,'tp'=8] {'tp'}, use_global_device_ids=true, to_apply=%region_33.34 | all-reduce | flops 128 | bytes 1024 | tf_op jit(solution)/shard_map/psum | solution.py:77
  272.6 0.8 fusion.34
  273.4 18.7 %all-gather.9.cloned.1.call-done = bf16[128,4096]{1,0:T(8,128)(2,1)} async-done(((bf16[128,512]{1,0:T(8,128)(2,1)}), bf16[128,4096]{1,0:T(8,128)(2,1)}) %all-gather.9.cloned.1.call-update) | async-done | bytes 1048592 | tf_op jit(solution)/shard_map/all_gather | solution.py:81
  292.1 6.7 %convolution_bitcast_fusion = f32[3,1,4,128,128]{3,4,2,1,0:T(8,128)S(1)} fusion(bf16[3,4,128,4096]{3,2,1,0:T(8,128)(2,1)} %bitcast.241, bf16[128,4096]{1,0:T(8,128)(2,1)} %all-gather.9.cloned.1.call-done), kind=kOutput, calls=%fused_computation.13 | convolution fusion | flops 1610612736 | bytes 14417920 | tf_op jit(solution)/shard_map/bsd,dce->bsce/dot_general | solution.py:83
  299.0 10.0 %all_gather.22 = bf16[1,4,512,128]{2,3,1,0:T(8,128)(2,1)S(1)} all-gather(bf16[1,4,128,128]{2,3,1,0:T(8,128)(2,1)S(1)} %pad_maximum_fusion.1), channel_id=1, replica_groups=mesh['seq'=4,'tp'=8] {'seq'}, dimensions={2}, use_global_device_ids=true | all-gather | bytes 655360 | tf_op jit(solution)/shard_map/all_gather | solution.py:94
  309.5 10.8 %all-gather.3 = bf16[1,1,4,512,128]{3,4,2,1,0:T(8,128)(2,1)S(1)} all-gather(bf16[1,1,4,128,128]{3,4,2,1,0:T(8,128)(2,1)S(1)} %slice.564), channel_id=5, replica_groups=mesh['seq'=4,'tp'=8] {'seq'}, dimensions={3}, use_global_device_ids=true | all-gather | bytes 655360 | tf_op jit(solution)/shard_map/all_gather | solution.py:95
  321.1 1.7 fusion.1
  322.8 31.4 %reduce-scatter.5.cloned.1.call-done = bf16[1,128,512]{2,1,0:T(8,128)(2,1)} async-done(((bf16[1,128,4096]{2,1,0:T(8,128)(2,1)}), bf16[1,128,512]{2,1,0:T(8,128)(2,1)}) %reduce-scatter.5.cloned.1.call-update) | async-done | bytes 131088 | tf_op jit(solution)/shard_map/reduce_scatter | solution.py:122
  354.2 1.0 multiply_reduce_fusion
  355.3 13.8 %psum.90 = f32[1,128]{1,0:T(1,128)S(1)} all-reduce(f32[1,128]{1,0:T(1,128)S(1)} %bitcast.257), channel_id=1, replica_groups=mesh['seq'=4,'tp'=8] {'tp'}, use_global_device_ids=true, to_apply=%region_38.39 | all-reduce | flops 128 | bytes 1024 | tf_op jit(solution)/shard_map/psum | solution.py:128
  369.1 1.7 multiply_multiply_fusion
  (125 shorter events, 21.1 us)
Async XLA Ops:
  7.2 118.5 %all-gather.7.cloned.1.call-start = ((), (), s32[]{:S(2)}) async-start(), calls=%async_computation.4 | async-start | bytes 1179648 | tf_op jit(solution)/shard_map/all_gather | solution.py:81
  9.2 1.1 copy-start.3
  11.3 75.4 %copy-start.2 = (f32[5,1,128,512]{3,2,1,0:T(8,128)S(1)}, f32[5,1,128,512]{3,2,1,0:T(8,128)}, u32[]{:S(2)}) copy-start(f32[5,1,128,512]{3,2,1,0:T(8,128)} %param.33) | copy-start | bytes 3932164
  16.3 88.2 %copy-start.11 = (f32[512]{0:T(512)S(1)}, f32[512]{0:T(512)}, u32[]{:S(2)}) copy-start(f32[512]{0:T(512)} %param.30) | copy-start | bytes 6148
  105.2 82.9 %reduce-scatter.3.cloned.1.call-start = ((), (), s32[]{:S(2)}) async-start(), calls=%async_computation.2 | async-start | bytes 1179648 | tf_op jit(solution)/shard_map/reduce_scatter | solution.py:122
  143.0 11.8 %copy-start = (bf16[512,4096]{1,0:T(8,128)(2,1)S(1)}, bf16[512,4096]{1,0:T(8,128)(2,1)}, u32[]{:S(2)}) copy-start(bf16[512,4096]{1,0:T(8,128)(2,1)} %param.29) | copy-start | bytes 12582916
  156.6 1.7 copy-start.4
  156.6 135.5 %all-gather.9.cloned.1.call-start = ((), (), s32[]{:S(2)}) async-start(), calls=%async_computation.5 | async-start | bytes 1179648 | tf_op jit(solution)/shard_map/all_gather | solution.py:81
  156.7 31.4 %copy-start.6 = (bf16[1,128,512]{2,1,0:T(8,128)(2,1)S(1)}, bf16[1,128,512]{2,1,0:T(8,128)(2,1)}, u32[]{:S(2)}) copy-start(bf16[1,128,512]{2,1,0:T(8,128)(2,1)} %param.27) | copy-start | bytes 393220
  156.7 31.4 %copy-start.10 = (f32[512]{0:T(512)S(1)}, f32[512]{0:T(512)}, u32[]{:S(2)}) copy-start(f32[512]{0:T(512)} %param.31) | copy-start | bytes 6148
  159.4 35.8 %copy-start.8 = (f32[4,128,512]{2,1,0:T(8,128)S(1)}, f32[4,128,512]{2,1,0:T(8,128)}, u32[]{:S(2)}) copy-start(f32[4,128,512]{2,1,0:T(8,128)} %slice_bitcast_fusion) | copy-start | bytes 3145732
  189.2 66.2 %copy-start.9 = (bf16[1,128,512]{2,1,0:T(8,128)(2,1)S(1)}, bf16[1,128,512]{2,1,0:T(8,128)(2,1)}, u32[]{:S(2)}) copy-start(bf16[1,128,512]{2,1,0:T(8,128)(2,1)} %reduce-scatter.3.cloned.1.call-done) | copy-start | bytes 393220
  189.2 66.3 %copy-start.5 = (f32[4,1,128,512]{3,2,1,0:T(8,128)S(1)}, f32[4,1,128,512]{3,2,1,0:T(8,128)}, u32[]{:S(2)}) copy-start(f32[4,1,128,512]{3,2,1,0:T(8,128)} %slice.432) | copy-start | bytes 3145732
  258.9 39.8 %copy-start.7 = (f32[1,128,512]{2,1,0:T(8,128)}, f32[1,128,512]{2,1,0:T(8,128)S(1)}, u32[]{:S(2)}) copy-start(f32[1,128,512]{2,1,0:T(8,128)S(1)} %get-tuple-element.153) | copy-start | bytes 786436
  273.3 80.9 %reduce-scatter.5.cloned.1.call-start = ((), (), s32[]{:S(2)}) async-start(), calls=%async_computation.3 | async-start | bytes 1179648 | tf_op jit(solution)/shard_map/reduce_scatter | solution.py:122
  309.4 11.6 %copy-start.1 = (bf16[512,4096]{1,0:T(8,128)(2,1)S(1)}, bf16[512,4096]{1,0:T(8,128)(2,1)}, u32[]{:S(2)}) copy-start(bf16[512,4096]{1,0:T(8,128)(2,1)} %param.29) | copy-start | bytes 12582916
Sparse Core Ops, SparseCore 0:
  105.4 20.2 all-gather.6
  156.7 31.3 reduce-scatter.2
  273.5 18.5 all-gather.8
  322.9 31.2 reduce-scatter.4
where the time goes:
time: 379 us; the launch traced here: 377 us
  blocking collectives  151 us (40%)
  waiting for transfers between devices  81.9 us (22%)
  matrix products  40.5 us (11%)
  local copies, waits for them, and re-layouts  35.5 us (9%)
  between operations  34.9 us (9%)
  other arithmetic  33.6 us (9%)
    reduce_scatter x2, waiting for transfers between devices, shards(): lax.psum_scatter(partial_value.astype(jnp.bfloat16), 'tp', scatter_dimens...  60.1 us
    psum x1, blocking collectives, shards(): gram = lax.psum(pair_products(residuals, residuals), ('seq', 'tp'))  42 us
    psum x2, blocking collectives, shards(): layer_squares = lax.psum(jnp.sum(mixed * mixed, axis=-1), 'tp')  28 us
    all_gather x2, blocking collectives, shards(): value_piece = lax.all_gather(value_rows, 'seq', axis=2, tiled=True)  21.8 us
    all_gather x2, waiting for transfers between devices, shards(): piece = lax.all_gather(normed, 'tp', axis=2, tiled=True)  21.8 us
    all_gather x2, blocking collectives, shards(): key_piece = lax.all_gather(key_rows, 'seq', axis=2, tiled=True)  20 us
    dot_general x1, local copies, waits for them, and re-layouts, shards(): jnp.einsum('bsd,dce->bsce', piece, rows, preferred_element_type=jnp.float32)  17 us
    psum x1, blocking collectives, shards(): lax.psum((jnp.sum(layer_summed * layer_summed, axis=-1), cross_scaled, cr...  13.9 us
  transfers between devices with their start and end apart: 4, of which 4 were waited for; matrix products, arithmetic and copies ran while one was open for 5% of the time, Pallas kernels for 0%

commit v1 on v0

--- a/solution.py
+++ b/solution.py
@@ -68,7 +68,8 @@
     positions = query_index.astype(jnp.float32)
     score_scale = HEAD_SIZE ** (-0.5)
     residuals = images - iterates
-    gram = lax.psum(pair_products(residuals, residuals), ("seq", "tp"))
+    partial = lax.psum(pair_products(residuals, residuals), "tp")
+    gram = lax.psum(partial, "seq")
     mixed = iterates[0]
     image = images[0]
     for step_index in range(ITERS):

time: 379 us -> 362 us (0.955)
  blocking collectives: 151 us -> 136 us
    psum x1 -> x2, blocking collectives: 42 us -> 28.1 us  [the longest x1 18.2 us: shards(): partial = lax.psum(pair_products(residuals, residuals), 'tp')]
where the time goes in v1:
time: 362 us; the launch traced here: 361 us
  blocking collectives  136 us (38%)
  waiting for transfers between devices  80.1 us (22%)
  matrix products  40.5 us (11%)
  local copies, waits for them, and re-layouts  35.5 us (10%)
  between operations  34.9 us (10%)
  other arithmetic  33.6 us (9%)
    reduce_scatter x2, waiting for transfers between devices, shards(): lax.psum_scatter(partial_value.astype(jnp.bfloat16), 'tp', scatter_dimens...  60 us
    psum x2, blocking collectives, shards(): layer_squares = lax.psum(jnp.sum(mixed * mixed, axis=-1), 'tp')  27.2 us
    all_gather x2, blocking collectives, shards(): value_piece = lax.all_gather(value_rows, 'seq', axis=2, tiled=True)  21.8 us
    all_gather x2, waiting for transfers between devices, shards(): piece = lax.all_gather(normed, 'tp', axis=2, tiled=True)  20.1 us
    all_gather x2, blocking collectives, shards(): key_piece = lax.all_gather(key_rows, 'seq', axis=2, tiled=True)  20 us
    psum x1, blocking collectives, shards(): partial = lax.psum(pair_products(residuals, residuals), 'tp')  18.2 us
    dot_general x1, local copies, waits for them, and re-layouts, shards(): jnp.einsum('bsd,dce->bsce', piece, rows, preferred_element_type=jnp.float32)  17 us
    psum x1, blocking collectives, shards(): lax.psum((jnp.sum(layer_summed * layer_summed, axis=-1), cross_scaled, cr...  14.1 us
  transfers between devices with their start and end apart: 4, of which 4 were waited for; matrix products, arithmetic and copies ran while one was open for 5% of the time, Pallas kernels for 0%

profile of v1, /device:TPU:0, one launch (start us, length us, event | category | flops | bytes accessed | tf_op | source)
XLA Modules:
  0.0 361.0 jit_solution(4377590714567800945)
XLA Ops:
  7.2 2.0 sub.129
  9.2 1.1 copy-done.3
  10.3 1.0 copy.29
  11.3 5.0 %convolution_bitcast_fusion.1 = f32[5,5]{1,0:T(8,128)S(1)} fusion(f32[5,128,512]{1,0,2:T(8,128)S(1)} %copy.29), kind=kOutput, calls=%fused_computation.18 | convolution fusion | flops 19660800 | bytes 1310820 | tf_op jit(solution)/shard_map/mbsd,nbsd->mn/dot_general | solution.py:53
  16.3 18.2 %psum.87 = f32[5,5]{1,0:T(8,128)S(1)} all-reduce(f32[5,5]{1,0:T(8,128)S(1)} %convolution_bitcast_fusion.1), channel_id=1, replica_groups=mesh['seq'=4,'tp'=8] {'tp'}, use_global_device_ids=true, to_apply=%region_0.0 | all-reduce | flops 25 | bytes 200 | tf_op jit(solution)/shard_map/psum | solution.py:71
  34.5 9.9 %psum.88 = f32[5,5]{1,0:T(8,128)S(1)} all-reduce(f32[5,5]{1,0:T(8,128)S(1)} %psum.87), channel_id=1, replica_groups=mesh['seq'=4,'tp'=8] {'seq'}, use_global_device_ids=true, to_apply=%region_1.0 | all-reduce | flops 25 | bytes 200 | tf_op jit(solution)/shard_map/psum | solution.py:72
  46.2 0.8 fusion.53
  47.7 0.8 select_reduce_fusion.9
  49.2 0.8 select_reduce_fusion.8
  50.7 0.8 select_reduce_fusion.7
  52.2 0.8 select_reduce_fusion.6
  53.1 0.7 fusion.102
  54.9 0.6 fusion.66
  56.2 0.6 fusion.70
  57.4 0.6 fusion.74
  58.6 0.6 fusion.78
  59.3 0.7 fusion.104
  61.9 0.7 fusion.90
  64.5 0.7 fusion.89
  72.9 3.2 fusion.4
  76.2 13.6 %psum.89 = f32[1,128]{1,0:T(1,128)S(1)} all-reduce(f32[1,128]{1,0:T(1,128)S(1)} %bitcast.256), channel_id=1, replica_groups=mesh['seq'=4,'tp'=8] {'tp'}, use_global_device_ids=true, to_apply=%region_10.11 | all-reduce | flops 128 | bytes 1024 | tf_op jit(solution)/shard_map/psum | solution.py:78
  89.8 0.8 fusion.38
  90.7 17.0 %copy.54 = bf16[3,512,4096]{2,1,0:T(8,128)(2,1)} copy(bf16[3,512,4096]{1,2,0:T(8,128)(2,1)} %bitcast.243) | data formatting | bytes 25165824 | tf_op jit(solution)/shard_map/bsd,dce->bsce/dot_general | solution.py:84
  107.9 1.4 all-gather.7.cloned.1.call-done
  109.3 6.7 %fusion.11 = f32[128,3,4,128]{0,3,2,1:T(8,128)S(1)} fusion(bf16[3,4,128,4096]{3,2,1,0:T(8,128)(2,1)} %bitcast.240, bf16[128,4096]{1,0:T(8,128)(2,1)} %all-gather.7.cloned.1.call-done), kind=kOutput, calls=%fused_computation.21 | convolution fusion | flops 1610612736 | bytes 14417920 | tf_op jit(solution)/shard_map/bsd,dce->bsce/dot_general | solution.py:84
  116.2 10.0 %all_gather.19 = bf16[1,4,512,128]{2,3,1,0:T(8,128)(2,1)S(1)} all-gather(bf16[1,4,128,128]{2,3,1,0:T(8,128)(2,1)S(1)} %pad_maximum_fusion), channel_id=1, replica_groups=mesh['seq'=4,'tp'=8] {'seq'}, dimensions={2}, use_global_device_ids=true | all-gather | bytes 655360 | tf_op jit(solution)/shard_map/all_gather | solution.py:95
  126.7 11.0 %all-gather.1 = bf16[1,1,4,512,128]{3,4,2,0,1:T(8,128)(2,1)S(1)} all-gather(bf16[1,1,4,128,128]{3,4,2,0,1:T(8,128)(2,1)S(1)} %slice.565), channel_id=3, replica_groups=mesh['seq'=4,'tp'=8] {'seq'}, dimensions={3}, use_global_device_ids=true | all-gather | bytes 655360 | tf_op jit(solution)/shard_map/all_gather | solution.py:96
  138.5 1.7 fusion
  140.4 1.0 slice.432
  141.9 1.1 slice_bitcast_fusion
  143.0 28.6 %reduce-scatter.3.cloned.1.call-done = bf16[1,128,512]{2,1,0:T(8,128)(2,1)} async-done(((bf16[1,128,4096]{2,1,0:T(8,128)(2,1)}), bf16[1,128,512]{2,1,0:T(8,128)(2,1)}) %reduce-scatter.3.cloned.1.call-update) | async-done | bytes 131088 | tf_op jit(solution)/shard_map/reduce_scatter | solution.py:123
  171.6 1.1 multiply_reduce_fusion.2
  172.8 5.9 %fusion.15 = f32[128,1,4]{2,1,0:T(1,128)S(1)} fusion(f32[4,128,512]{2,1,0:T(8,128)} %slice_bitcast_fusion, f32[128,512,1]{1,0,2:T(8,128)S(1)} %get-tuple-element.164), kind=kOutput, calls=%fused_computation.27 | convolution fusion | flops 3145728 | bytes 1312768 | tf_op jit(solution)/shard_map/bsd,mbsd->mbs/dot_general | solution.py:135
  178.7 4.6 %fusion.13 = f32[128,1,4]{2,1,0:T(1,128)S(1)} fusion(f32[4,128,512]{2,1,0:T(8,128)S(1)} %copy-done.8, f32[128,512,1]{1,0,2:T(8,128)S(1)} %get-tuple-element.165), kind=kOutput, calls=%fused_computation.25 | convolution fusion | flops 3145728 | bytes 1312768 | tf_op jit(solution)/shard_map/bsd,mbsd->mbs/dot_general | solution.py:138
  183.4 14.1 %all-reduce.2 = (f32[1,128]{1,0:T(1,128)S(1)}, f32[1,128]{1,0:T(1,128)S(1)}, f32[1,128]{1,0:T(1,128)S(1)}, f32[4,1,128]{2,0,1:T(4,128)S(1)}, f32[4,1,128]{2,0,1:T(4,128)S(1)}) all-reduce(f32[1,128]{1,0:T(1,128)S(1)} %bitcast.254, f32[1,128]{1,0:T(1,128)S(1)} %bitcast.253, ...), channel_id=1, replica_groups=mesh['seq'=4,'tp'=8] {'tp'}, use_global_device_ids=true, to_apply=%region_15.16 | all-reduce | flops 1408 | bytes 11264 | tf_op jit(solution)/shard_map/psum | solution.py:139
  198.2 11.0 %all-reduce.3 = (f32[1]{0:T(128)}, f32[4]{0:T(128)S(1)}) all-reduce(f32[1]{0:T(128)} %bitcast.72, f32[4]{0:T(128)S(1)} %subtract_reduce_fusion), channel_id=1, replica_groups=mesh['seq'=4,'tp'=8] {'seq'}, use_global_device_ids=true, to_apply=%region_25.26 | all-reduce | flops 5 | bytes 40 | tf_op jit(solution)/shard_map/psum | solution.py:157
  209.3 0.7 maximum_bitcast_fusion.1
  210.0 0.7 select_reduce_fusion.5
  211.9 0.8 fusion.58
  213.4 0.8 select_reduce_fusion.3
  214.9 0.8 select_reduce_fusion.2
  216.4 0.8 select_reduce_fusion.1
  217.9 0.8 select_reduce_fusion
  218.8 0.7 fusion.101
  220.7 0.6 fusion.68
  221.9 0.6 fusion.72
  223.2 0.6 fusion.76
  224.4 0.6 fusion.80
  225.1 0.6 fusion.103
  227.6 0.8 fusion.85
  230.5 0.7 fusion.84
  233.2 0.7 fusion.83
  239.3 3.2 fusion.2
  242.6 13.6 %psum.97 = f32[1,128]{1,0:T(1,128)S(1)} all-reduce(f32[1,128]{1,0:T(1,128)S(1)} %bitcast.255), channel_id=1, replica_groups=mesh['seq'=4,'tp'=8] {'tp'}, use_global_device_ids=true, to_apply=%region_34.35 | all-reduce | flops 128 | bytes 1024 | tf_op jit(solution)/shard_map/psum | solution.py:78
  256.2 0.8 fusion.34
  257.0 18.7 %all-gather.9.cloned.1.call-done = bf16[128,4096]{1,0:T(8,128)(2,1)} async-done(((bf16[128,512]{1,0:T(8,128)(2,1)}), bf16[128,4096]{1,0:T(8,128)(2,1)}) %all-gather.9.cloned.1.call-update) | async-done | bytes 1048592 | tf_op jit(solution)/shard_map/all_gather | solution.py:82
  275.7 6.7 %convolution_bitcast_fusion = f32[3,1,4,128,128]{3,4,2,1,0:T(8,128)S(1)} fusion(bf16[3,4,128,4096]{3,2,1,0:T(8,128)(2,1)} %bitcast.241, bf16[128,4096]{1,0:T(8,128)(2,1)} %all-gather.9.cloned.1.call-done), kind=kOutput, calls=%fused_computation.13 | convolution fusion | flops 1610612736 | bytes 14417920 | tf_op jit(solution)/shard_map/bsd,dce->bsce/dot_general | solution.py:84
  282.6 10.0 %all_gather.22 = bf16[1,4,512,128]{2,3,1,0:T(8,128)(2,1)S(1)} all-gather(bf16[1,4,128,128]{2,3,1,0:T(8,128)(2,1)S(1)} %pad_maximum_fusion.1), channel_id=1, replica_groups=mesh['seq'=4,'tp'=8] {'seq'}, dimensions={2}, use_global_device_ids=true | all-gather | bytes 655360 | tf_op jit(solution)/shard_map/all_gather | solution.py:95
  293.1 10.8 %all-gather.3 = bf16[1,1,4,512,128]{3,4,2,1,0:T(8,128)(2,1)S(1)} all-gather(bf16[1,1,4,128,128]{3,4,2,1,0:T(8,128)(2,1)S(1)} %slice.564), channel_id=5, replica_groups=mesh['seq'=4,'tp'=8] {'seq'}, dimensions={3}, use_global_device_ids=true | all-gather | bytes 655360 | tf_op jit(solution)/shard_map/all_gather | solution.py:96
  304.7 1.7 fusion.1
  306.5 31.4 %reduce-scatter.5.cloned.1.call-done = bf16[1,128,512]{2,1,0:T(8,128)(2,1)} async-done(((bf16[1,128,4096]{2,1,0:T(8,128)(2,1)}), bf16[1,128,512]{2,1,0:T(8,128)(2,1)}) %reduce-scatter.5.cloned.1.call-update) | async-done | bytes 131088 | tf_op jit(solution)/shard_map/reduce_scatter | solution.py:123
  337.9 1.0 multiply_reduce_fusion
  338.9 13.8 %psum.98 = f32[1,128]{1,0:T(1,128)S(1)} all-reduce(f32[1,128]{1,0:T(1,128)S(1)} %bitcast.257), channel_id=1, replica_groups=mesh['seq'=4,'tp'=8] {'tp'}, use_global_device_ids=true, to_apply=%region_39.40 | all-reduce | flops 128 | bytes 1024 | tf_op jit(solution)/shard_map/psum | solution.py:129
  352.7 1.7 multiply_multiply_fusion
  (126 shorter events, 21.8 us)
Async XLA Ops:
  7.2 102.2 %all-gather.7.cloned.1.call-start = ((), (), s32[]{:S(2)}) async-start(), calls=%async_computation.4 | async-start | bytes 1179648 | tf_op jit(solution)/shard_map/all_gather | solution.py:82
  9.2 1.1 copy-start.3
  11.3 61.6 %copy-start.2 = (f32[5,1,128,512]{3,2,1,0:T(8,128)S(1)}, f32[5,1,128,512]{3,2,1,0:T(8,128)}, u32[]{:S(2)}) copy-start(f32[5,1,128,512]{3,2,1,0:T(8,128)} %param.33) | copy-start | bytes 3932164
  16.3 73.5 %copy-start.11 = (f32[512]{0:T(512)S(1)}, f32[512]{0:T(512)}, u32[]{:S(2)}) copy-start(f32[512]{0:T(512)} %param.30) | copy-start | bytes 6148
  90.6 81.0 %reduce-scatter.3.cloned.1.call-start = ((), (), s32[]{:S(2)}) async-start(), calls=%async_computation.2 | async-start | bytes 1179648 | tf_op jit(solution)/shard_map/reduce_scatter | solution.py:123
  126.7 11.8 %copy-start = (bf16[512,4096]{1,0:T(8,128)(2,1)S(1)}, bf16[512,4096]{1,0:T(8,128)(2,1)}, u32[]{:S(2)}) copy-start(bf16[512,4096]{1,0:T(8,128)(2,1)} %param.29) | copy-start | bytes 12582916
  140.2 1.7 copy-start.4
  140.3 135.5 %all-gather.9.cloned.1.call-start = ((), (), s32[]{:S(2)}) async-start(), calls=%async_computation.5 | async-start | bytes 1179648 | tf_op jit(solution)/shard_map/all_gather | solution.py:82
  140.4 31.3 %copy-start.6 = (bf16[1,128,512]{2,1,0:T(8,128)(2,1)S(1)}, bf16[1,128,512]{2,1,0:T(8,128)(2,1)}, u32[]{:S(2)}) copy-start(bf16[1,128,512]{2,1,0:T(8,128)(2,1)} %param.27) | copy-start | bytes 393220
  140.4 31.3 %copy-start.10 = (f32[512]{0:T(512)S(1)}, f32[512]{0:T(512)}, u32[]{:S(2)}) copy-start(f32[512]{0:T(512)} %param.31) | copy-start | bytes 6148
  143.0 35.7 %copy-start.8 = (f32[4,128,512]{2,1,0:T(8,128)S(1)}, f32[4,128,512]{2,1,0:T(8,128)}, u32[]{:S(2)}) copy-start(f32[4,128,512]{2,1,0:T(8,128)} %slice_bitcast_fusion) | copy-start | bytes 3145732
  172.7 66.3 %copy-start.9 = (bf16[1,128,512]{2,1,0:T(8,128)(2,1)S(1)}, bf16[1,128,512]{2,1,0:T(8,128)(2,1)}, u32[]{:S(2)}) copy-start(bf16[1,128,512]{2,1,0:T(8,128)(2,1)} %reduce-scatter.3.cloned.1.call-done) | copy-start | bytes 393220
  172.7 66.4 %copy-start.5 = (f32[4,1,128,512]{3,2,1,0:T(8,128)S(1)}, f32[4,1,128,512]{3,2,1,0:T(8,128)}, u32[]{:S(2)}) copy-start(f32[4,1,128,512]{3,2,1,0:T(8,128)} %slice.432) | copy-start | bytes 3145732
  242.6 39.9 %copy-start.7 = (f32[1,128,512]{2,1,0:T(8,128)}, f32[1,128,512]{2,1,0:T(8,128)S(1)}, u32[]{:S(2)}) copy-start(f32[1,128,512]{2,1,0:T(8,128)S(1)} %get-tuple-element.153) | copy-start | bytes 786436
  257.0 80.9 %reduce-scatter.5.cloned.1.call-start = ((), (), s32[]{:S(2)}) async-start(), calls=%async_computation.3 | async-start | bytes 1179648 | tf_op jit(solution)/shard_map/reduce_scatter | solution.py:123
  293.1 11.6 %copy-start.1 = (bf16[512,4096]{1,0:T(8,128)(2,1)S(1)}, bf16[512,4096]{1,0:T(8,128)(2,1)}, u32[]{:S(2)}) copy-start(bf16[512,4096]{1,0:T(8,128)(2,1)} %param.29) | copy-start | bytes 12582916
Sparse Core Ops, SparseCore 0:
  90.7 18.5 all-gather.6
  140.4 31.2 reduce-scatter.2
  257.1 18.5 all-gather.8
  306.6 31.2 reduce-scatter.4
